TPU v7x, 128 devices: a whole 4x4x4 slice. The times are simulated.
128 devices in a mesh: dp: 128 (over z, y, x, core).
Axes of the slice: x: 4, y: 4, z: 4, core: 2. Of those that a mesh axis runs over, the one named last changes fastest.
Arguments:
- queries: bfloat16 [8192, 2048], P('dp'), may hold values from -6 to 6
- new_kv: bfloat16 [2, 8192, 256], P(None, 'dp'), may hold values from -6 to 6
- residual: bfloat16 [8192, 2048], P('dp'), may hold values from -6 to 6
- prefix_cache: bfloat16 [2, 128, 1024, 256], P(None, 'dp'), may hold values from -6 to 6
- prefix_len: int32 [128], P('dp'), may hold values from 0 to 1024, as said below
- decode_cache: bfloat16 [2, 512, 1024, 256], P(None, 'dp'), may hold values from -6 to 6
- cache_len: int32 [512], P('dp'), may hold values from 1 to 1024, as said below
- placement: int32 [512], replicated, may hold values from 0 to 511, each once
- w_out: bfloat16 [2048, 2048], replicated, may hold values from -0.125 to 0.125
- norm_gain: bfloat16 [2048], replicated, may hold values from 0.099609375 to 1.8984375
- routes: int32 [8192, 8], P('dp'), may hold values from 0 to 127, all different within a row; in each aligned block of 64 rows (0 to 63, 64 to 127, ...) at most 8 rows name the same one
- route_weight: float32 [8192, 8], P('dp'), may hold values from 0.03 to 0.3
- w_gate: bfloat16 [128, 2048, 768], P('dp'), may hold values from -0.125 to 0.125
- w_up: bfloat16 [128, 2048, 768], P('dp'), may hold values from -0.125 to 0.125
- w_down: bfloat16 [128, 768, 2048], P('dp'), may hold values from -0.21875 to 0.21875
Outputs:
- mixed: bfloat16 [8192, 2048], P('dp')
Inputs may be any that keep to these rules, and one draw needn't show every extreme that they name: `routes`: in the rows of one device (aligned blocks of 64 rows) no expert is named by more than 8 rows, a bound that some block reaches. `cache_len`: some slot holds 1024 cached tokens. `prefix_len`: some device's prefill request has 1024 earlier tokens. `placement`: every slot holds exactly one request.
All inputs are finite; a program needn't handle non-finite values.
Results may differ from a plain program's by a relative error of at most 0.014.
Values may be sent and summed in bfloat16 or wider, within the bound.
A program may use at most 128 MiB of HBM per device.

v0:
```python
import functools
import math

import jax
import jax.numpy as jnp
from jax import lax
from jax.experimental import pallas as pl
from jax.experimental.pallas import tpu as pltpu
from jax.sharding import PartitionSpec as P

HEAD = 128
MASKED = -1e30
EPSILON = 1e-06
MESH = pl.DeviceIdType.MESH
ORDERS = ((0, 1, 2), (1, 2, 0), (2, 0, 1))
STRIDES = (32, 8, 2)
DEC = 4
STRETCH = 60
GROUP = 8


def dot_t(a, b):
    return lax.dot_general(a, b, (((1,), (1,)), ((), ())), preferred_element_type=jnp.float32)


def dot_n(a, b):
    return lax.dot_general(a, b, (((1,), (0,)), ((), ())), preferred_element_type=jnp.float32)


class Gather:
    def __init__(self, me, sources, buffers, send_sem, recv_sem, local_sem):
        self.me = me
        self.coords = (me // 32, (me // 8) % 4, (me // 2) % 4)
        self.core = me % 2
        self.sources, self.buffers = sources, buffers
        self.send_sem, self.recv_sem, self.local_sem = send_sem, recv_sem, local_sem
        self.started = []

    def slot(self, buffer, gathered):
        index = tuple(
            slice(None) if axis in gathered else self.coords[axis] for axis in range(3)
        )
        return buffer.at[index + (self.core,)]

    def start(self, phase):
        started = []
        for p, (source, buffer) in enumerate(zip(self.sources, self.buffers)):
            order = ORDERS[p]
            if phase == 0:
                own = pltpu.make_async_copy(source, self.slot(buffer, ()), self.local_sem.at[p])
                own.start()
                started.append(own)
            if phase < 3:
                here = self.slot(buffer, order[:phase])
                axis = order[phase]
                for d in range(1, 4):
                    peer = self.me + ((self.coords[axis] + d) % 4 - self.coords[axis]) * STRIDES[axis]
                    copy = pltpu.make_async_remote_copy(
                        src_ref=source if phase == 0 else here,
                        dst_ref=here,
                        send_sem=self.send_sem.at[p, phase * 3 + d - 1],
                        recv_sem=self.recv_sem.at[p, phase * 3 + d - 1],
                        device_id=(peer,),
                        device_id_type=MESH,
                    )
                    copy.start()
                    started.append(copy)
            else:
                here = self.slot(buffer, (0, 1, 2))
                copy = pltpu.make_async_remote_copy(
                    src_ref=here,
                    dst_ref=here,
                    send_sem=self.send_sem.at[p, 9],
                    recv_sem=self.recv_sem.at[p, 9],
                    device_id=(self.me + 1 - 2 * self.core,),
                    device_id_type=MESH,
                )
                copy.start()
                started.append(copy)
        self.started = started

    def finish(self):
        for copy in self.started:
            copy.wait()
        self.started = []


def attention_kernel(
    index_ref, len_ref, q_ref, kv_ref, res_ref, gain_ref, q0_ref, q1_ref, pair_ref,
    prefix_hbm, cache_hbm, wout_hbm,
    hidden_ref, normed_ref,
    prefix, cache, wout, att, a0, a1, a2, b0, b1, s0, s1,
    load_sem, send_a, recv_a, local_a, send_b, recv_b, local_b,
):
    me = lax.axis_index("dp")
    loads = [
        pltpu.make_async_copy(prefix_hbm, prefix, load_sem.at[0]),
        pltpu.make_async_copy(cache_hbm, cache, load_sem.at[1]),
        pltpu.make_async_copy(wout_hbm, wout, load_sem.at[2]),
    ]
    for copy in loads:
        copy.start()
    first = Gather(me, (q0_ref, q1_ref, pair_ref), (a0, a1, a2), send_a, recv_a, local_a)
    second = Gather(me, (s0, s1), (b0, b1), send_b, recv_b, local_b)
    barrier = pltpu.get_barrier_semaphore()
    for axis in range(3):
        for d in range(1, 4):
            peer = me + ((first.coords[axis] + d) % 4 - first.coords[axis]) * STRIDES[axis]
            pl.semaphore_signal(barrier, inc=1, device_id=(peer,), device_id_type=MESH)
    pl.semaphore_signal(
        barrier, inc=1, device_id=(me + 1 - 2 * first.core,), device_id_type=MESH
    )
    pl.semaphore_wait(barrier, 10)
    scale = 1.0 / math.sqrt(HEAD)
    rows = q_ref.shape[0]
    cache_rows = prefix.shape[2 - 1]

    def prefill(part):
        g, half = part // 2, part % 2
        heads = [g * GROUP + half * 4 + j for j in range(4)]
        q = jnp.concatenate([q_ref[:, h * HEAD:(h + 1) * HEAD] for h in heads], axis=0)
        cols = slice(g * HEAD, (g + 1) * HEAD)
        old = dot_t(q, prefix[0, :, cols]) * scale
        new = dot_t(q, kv_ref[0, :, cols]) * scale
        position = lax.broadcasted_iota(jnp.int32, old.shape, 1)
        old = jnp.where(position < len_ref[DEC], old, MASKED)
        row = lax.broadcasted_iota(jnp.int32, new.shape, 0) % rows
        new = jnp.where(lax.broadcasted_iota(jnp.int32, new.shape, 1) <= row, new, MASKED)
        top = jnp.maximum(old.max(axis=-1, keepdims=True), new.max(axis=-1, keepdims=True))
        old, new = jnp.exp(old - top), jnp.exp(new - top)
        inv = 1.0 / (old.sum(axis=-1, keepdims=True) + new.sum(axis=-1, keepdims=True))
        out = dot_n((old * inv).astype(jnp.bfloat16), prefix[1, :, cols])
        out += dot_n((new * inv).astype(jnp.bfloat16), kv_ref[1, :, cols])
        for j, h in enumerate(heads):
            att[:, h * HEAD:(h + 1) * HEAD] = out[j * rows:(j + 1) * rows]

    first.start(0)
    loads[0].wait()
    prefill(0)
    first.finish()
    first.start(1)
    prefill(1)
    first.finish()
    first.start(2)
    prefill(2)
    first.finish()
    first.start(3)
    loads[1].wait()
    first.finish()

    for s in range(DEC):
        src = index_ref[s]
        sz, sy, sx, sc = src // 128, (src // 32) % 4, (src // 8) % 4, (src // 4) % 2
        sr = src % 4
        pair = a2[sz, sy, sx, sc, sr].astype(jnp.float32)
        for g, (buf, out_ref) in enumerate(((a0, s0), (a1, s1))):
            q = buf[sz, sy, sx, sc, sr]
            cols = slice(g * HEAD, (g + 1) * HEAD)
            old = dot_t(q, cache[0, s, :, cols]) * scale
            new = (q.astype(jnp.float32) * pair[g:g + 1]).sum(axis=-1, keepdims=True) * scale
            position = lax.broadcasted_iota(jnp.int32, old.shape, 1)
            old = jnp.where(position < len_ref[s], old, MASKED)
            top = jnp.maximum(old.max(axis=-1, keepdims=True), new)
            old, new = jnp.exp(old - top), jnp.exp(new - top)
            inv = 1.0 / (old.sum(axis=-1, keepdims=True) + new)
            out = dot_n((old * inv).astype(jnp.bfloat16), cache[1, s, :, cols])
            own = (new * inv).astype(jnp.bfloat16).astype(jnp.float32)
            out_ref[s] = (out + own * pair[2 + g:3 + g]).astype(jnp.bfloat16)

    second.start(0)
    prefill(3)
    second.finish()
    second.start(1)
    loads[2].wait()
    second.finish()
    second.start(2)
    second.finish()
    second.start(3)
    second.finish()
    for s in range(DEC):
        src = index_ref[DEC + s]
        sz, sy, sx, sc = src // 128, (src // 32) % 4, (src // 8) % 4, (src // 4) % 2
        sr = src % 4
        for g, buf in enumerate((b0, b1)):
            out = buf[sz, sy, sx, sc, sr].astype(jnp.float32)
            for j in range(GROUP):
                h = g * GROUP + j
                att[STRETCH + s:STRETCH + s + 1, h * HEAD:(h + 1) * HEAD] = out[j:j + 1]

    attended = att[...].astype(jnp.bfloat16)
    step = 512
    total = jnp.zeros((rows, 1), jnp.float32)
    width = wout.shape[1]
    for n in range(0, width, step):
        piece = dot_n(attended, wout[:, n:n + step])
        piece = (piece + res_ref[:, n:n + step].astype(jnp.float32)).astype(jnp.bfloat16)
        hidden_ref[:, n:n + step] = piece
        piece = piece.astype(jnp.float32)
        total += (piece * piece).sum(axis=-1, keepdims=True)
    norm = lax.rsqrt(total * (1.0 / width) + EPSILON)
    normed_ref[...] = (
        hidden_ref[...].astype(jnp.float32) * norm * gain_ref[...].astype(jnp.float32)
    ).astype(jnp.bfloat16)


def attention(index, lens, queries, new_kv, residual, gain, q0, q1, pair, prefix, cache, w_out):
    rows, width = residual.shape
    vmem = pl.BlockSpec(memory_space=pltpu.VMEM)
    smem = pl.BlockSpec(memory_space=pltpu.SMEM)
    hbm = pl.BlockSpec(memory_space=pl.ANY)
    bf16 = jnp.bfloat16
    dma = pltpu.SemaphoreType.DMA
    return pl.pallas_call(
        attention_kernel,
        out_shape=[jax.ShapeDtypeStruct((rows, width), bf16)] * 2,
        in_specs=[smem, smem] + [vmem] * 7 + [hbm] * 3,
        out_specs=[vmem, vmem],
        scratch_shapes=[
            pltpu.VMEM(prefix.shape, bf16),
            pltpu.VMEM(cache.shape, bf16),
            pltpu.VMEM(w_out.shape, bf16),
            pltpu.VMEM((rows, queries.shape[1]), jnp.float32),
            pltpu.VMEM((4, 4, 4, 2) + q0.shape, bf16),
            pltpu.VMEM((4, 4, 4, 2) + q1.shape, bf16),
            pltpu.VMEM((4, 4, 4, 2) + pair.shape, bf16),
            pltpu.VMEM((4, 4, 4, 2) + q0.shape, bf16),
            pltpu.VMEM((4, 4, 4, 2) + q1.shape, bf16),
            pltpu.VMEM(q0.shape, bf16),
            pltpu.VMEM(q1.shape, bf16),
            dma((3,)),
            dma((3, 10)), dma((3, 10)), dma((3,)),
            dma((2, 10)), dma((2, 10)), dma((2,)),
        ],
        compiler_params=pltpu.CompilerParams(
            collective_id=0, has_side_effects=True, vmem_limit_bytes=56 * 2**20
        ),
        name="attention",
    )(index, lens, queries, new_kv, residual, gain, q0, q1, pair, prefix, cache, w_out)


def expert_rows(block, gate_w, up_w, down_w):
    block_shape = block.shape
    flat_rows = block.reshape(-1, block_shape[-1])
    gate_part = jnp.dot(flat_rows, gate_w[0], preferred_element_type=jnp.float32)
    up_part = jnp.dot(flat_rows, up_w[0], preferred_element_type=jnp.float32)
    act = (jax.nn.silu(gate_part) * up_part).astype(jnp.bfloat16)
    result = jnp.dot(act, down_w[0], preferred_element_type=jnp.float32).astype(jnp.bfloat16)
    return result.reshape(block_shape)


def local(
    queries, new_kv, residual, prefix_cache, prefix_len, decode_cache, cache_len, placement,
    w_out, norm_gain, routes, route_weight, w_gate, w_up, w_down,
):
    row_count, width = residual.shape
    experts = lax.axis_size("dp")
    capacity = max(2, 2 * row_count * routes.shape[1] // experts)
    me = lax.axis_index("dp")
    slot_ids = me * DEC + jnp.arange(DEC, dtype=jnp.int32)
    request_ids = jnp.arange(placement.shape[0], dtype=jnp.int32)
    matches = placement[None, :] == slot_ids[:, None]
    request = jnp.sum(jnp.where(matches, request_ids[None, :], 0), axis=1)
    my_slots = lax.dynamic_slice_in_dim(placement, me * DEC, DEC)
    index = jnp.concatenate([request, my_slots])
    lens = jnp.concatenate([cache_len, prefix_len])
    q = queries[STRETCH:].reshape(DEC, 2, GROUP, HEAD)
    pair = jnp.transpose(new_kv[:, STRETCH:].reshape(2, DEC, 2, HEAD), (1, 0, 2, 3))
    pair = pair.reshape(DEC, 4, HEAD)
    hidden_state, normed = attention(
        index, lens, queries, new_kv, residual, norm_gain.reshape(1, width), q[:, 0], q[:, 1], pair,
        prefix_cache[:, 0], decode_cache, w_out,
    )
    expert_ids = jnp.arange(experts, dtype=jnp.int32)
    named = routes[:, :, None] == expert_ids[None, None, :]
    member = jnp.any(named, axis=1)
    weight = jnp.sum(jnp.where(named, route_weight[:, :, None], 0.0), axis=1)
    row_ids = jnp.arange(row_count, dtype=jnp.int32)
    lower = (row_ids[None, :] < row_ids[:, None]).astype(jnp.bfloat16)
    rank = jnp.dot(lower, member.astype(jnp.bfloat16), preferred_element_type=jnp.float32)
    rank = jnp.where(member, rank, -1.0).T
    slots = jnp.arange(capacity, dtype=jnp.float32)
    chosen = rank[:, None, :] == slots[None, :, None]
    picks = chosen.reshape(experts * capacity, row_count)
    buffer = jnp.dot(picks.astype(jnp.bfloat16), normed, preferred_element_type=jnp.float32)
    buffer = buffer.astype(jnp.bfloat16).reshape(experts, capacity, width)
    arrived_rows = lax.all_to_all(buffer, "dp", split_axis=0, concat_axis=0, tiled=True)
    served = expert_rows(arrived_rows, w_gate, w_up, w_down)
    returned = lax.all_to_all(served, "dp", split_axis=0, concat_axis=0, tiled=True)
    mix = jnp.where(chosen, weight.T[:, None, :], 0.0).reshape(experts * capacity, row_count)
    high = lax.reduce_precision(mix, 8, 7)
    rest = (mix - high).astype(jnp.bfloat16)
    both = jnp.concatenate([high.astype(jnp.bfloat16), rest], axis=1)
    sums = lax.dot_general(
        both, returned.reshape(experts * capacity, width), (((0,), (0,)), ((), ())),
        preferred_element_type=jnp.float32,
    )
    mixed = hidden_state.astype(jnp.float32) + sums[:row_count] + sums[row_count:]
    return mixed.astype(jnp.bfloat16)


def solution(mesh):
    in_specs = (
        P("dp", None),
        P(None, "dp", None),
        P("dp", None),
        P(None, "dp", None, None),
        P("dp"),
        P(None, "dp", None, None),
        P("dp"),
        P(),
        P(),
        P(),
        P("dp", None),
        P("dp", None),
        P("dp", None, None),
        P("dp", None, None),
        P("dp", None, None),
    )
    out_specs = P("dp", None)
    return jax.shard_map(local, mesh=mesh, in_specs=in_specs, out_specs=out_specs, check_vma=False)
```

profile of v0, /device:TPU:1, one launch (start us, length us, event | category | flops | bytes accessed | tf_op | source)
XLA Modules:
  0.0 200.9 jit_solution(12708703486298047979)
XLA Ops:
  0.0 0.9 dynamic_slice.3
  0.9 0.9 select_reduce_fusion.1
  1.8 0.8 slice_bitcast_fusion
  2.6 0.6 slice_bitcast_fusion.1
  3.2 0.7 slice.21
  3.9 0.6 copy.28
  4.5 1.3 reshape.40.gain_ref
  6.5 0.8 copy.29
  7.3 0.2 fusion.24
  7.4 0.1 convolution_select_fusion
  7.8 0.6 pad_add_fusion.index_ref
  8.4 1.3 pad_add_fusion.1.len_ref
  9.6 49.3 %attention.1 = (bf16[64,2048]{1,0:T(8,128)(2,1)}, bf16[64,2048]{1,0:T(8,128)(2,1)}) custom-call(s32[8]{0:T(128)} %pad_add_fusion.index_ref, s32[5]{0:T(128)} %pad_add_fusion.1.len_ref, bf16[64,2048]{1,0:T(8,128)(2,1)} %q_ref.1, bf16[2,64,256]{2,1,0:T(8,128)(2,1)} %kv_ref.1, bf16[64,2048]{1,0:T(8,128)(2,1)} %res_ref.1, bf16[1,2048]{1,0:T(2,128)(2,1)} %reshape.40.gain_ref, ...), custom_call_target="tpu_custom_call" | custom-call | tf_op jit(solution)/shard_map/attention/pallas_call | solution.py:213
  58.9 2.2 %convert_bitcast_fusion.1 = bf16[128,8,2048]{2,1,0:T(8,128)(2,1)S(1)} fusion(bf16[64,2048]{1,0:T(8,128)(2,1)} %get-tuple-element.8, f32[1024]{0:T(1024)S(1)} %eq.56, f32[128,64]{1,0:T(8,128)S(1)} %copy.30), kind=kOutput, calls=%fused_computation.7 | convolution fusion | flops 270598144 | bytes 4493312 | tf_op jit(solution)/shard_map/dot_general | solution.py:284
  61.2 58.1 %all_to_all.10 = bf16[128,8,2048]{2,1,0:T(8,128)(2,1)S(1)} all-to-all(bf16[128,8,2048]{2,1,0:T(8,128)(2,1)S(1)} %convert_bitcast_fusion.1), channel_id=1, replica_groups=mesh['dp'=128] {'dp'}, dimensions={0} | all-to-all | bytes 8388608 | tf_op jit(solution)/shard_map/all_to_all | solution.py:286
  119.3 2.0 copy-done.1
  121.2 5.2 %fusion.4 = f32[1024,768]{1,0:T(8,128)} fusion(bf16[128,8,2048]{2,1,0:T(8,128)(2,1)S(1)} %all_to_all.10, bf16[1,2048,768]{2,1,0:T(8,128)(2,1)S(1)} %copy-done.4), kind=kOutput, calls=%fused_computation.4 | convolution fusion | flops 3221225472 | bytes 10485760 | tf_op jit(solution)/shard_map/dot_general | solution.py:244
  126.4 12.2 %convert_bitcast_fusion = bf16[128,8,2048]{2,1,0:T(8,128)(2,1)} fusion(bf16[1,768,2048]{2,1,0:T(8,128)(2,1)S(1)} %copy-done, f32[1024,768]{1,0:T(8,128)} %fusion.4, bf16[1,2048,768]{2,1,0:T(8,128)(2,1)} %param.28, bf16[128,8,2048]{2,1,0:T(8,128)(2,1)} %copy-done.1), kind=kOutput, calls=%fused_computation.6 | convolution fusion | flops 6449266688 | bytes 17825792 | tf_op jit(solution)/shard_map/dot_general | solution.py:247
  138.6 5.6 %all-to-all-start.1 = ((bf16[128,8,2048]{2,1,0:T(8,128)(2,1)}), bf16[128,8,2048]{2,1,0:T(8,128)(2,1)}, u32[]{:S(2)}, u32[]{:S(2)}) async-start(bf16[128,8,2048]{2,1,0:T(8,128)(2,1)} %convert_bitcast_fusion), calls=%async_computation.1 | async-start | bytes 8388608 | tf_op jit(solution)/shard_map/all_to_all | solution.py:288
  144.4 0.2 select_reduce_fusion
  144.7 0.9 reduce-precision_convert_fusion
  145.6 51.5 %all-to-all-done.1 = bf16[128,8,2048]{2,1,0:T(8,128)(2,1)} async-done(((bf16[128,8,2048]{2,1,0:T(8,128)(2,1)}), bf16[128,8,2048]{2,1,0:T(8,128)(2,1)}, u32[]{:S(2)}, u32[]{:S(2)}) %all-to-all-start.1) | async-done | bytes 4194336 | tf_op jit(solution)/shard_map/all_to_all | solution.py:288
  197.0 3.1 %fusion = f32[128,2048]{1,0:T(8,128)S(1)} fusion(bf16[128,8,2048]{2,1,0:T(8,128)(2,1)} %all-to-all-done.1, bf16[1024,64]{1,0:T(8,128)(2,1)} %get-tuple-element.10, bf16[1024,64]{1,0:T(8,128)(2,1)S(1)} %get-tuple-element.9), kind=kOutput, calls=%fused_computation | convolution fusion | flops 537395200 | bytes 5505024 | tf_op jit(solution)/shard_map/dot_general | solution.py:293
  200.2 0.8 fusion.18
  (17 shorter events, 0.4 us)
Async XLA Ops:
  0.0 126.4 %copy-start = (bf16[1,768,2048]{2,1,0:T(8,128)(2,1)S(1)}, bf16[1,768,2048]{2,1,0:T(8,128)(2,1)}, u32[]{:S(2)}) copy-start(bf16[1,768,2048]{2,1,0:T(8,128)(2,1)} %param.29) | copy-start | bytes 9437188
  61.1 60.1 %copy-start.4 = (bf16[1,2048,768]{2,1,0:T(8,128)(2,1)S(1)}, bf16[1,2048,768]{2,1,0:T(8,128)(2,1)}, u32[]{:S(2)}) copy-start(bf16[1,2048,768]{2,1,0:T(8,128)(2,1)} %param.27) | copy-start | bytes 9437188
  119.2 2.0 copy-start.1
  138.6 5.6 %copy-start.3 = (f32[64,8]{0,1:T(8,128)S(1)}, f32[64,8]{0,1:T(8,128)}, u32[]{:S(2)}) copy-start(f32[64,8]{0,1:T(8,128)} %param.26) | copy-start | bytes 6148
  138.6 58.4 %all-to-all-start.1 = ((bf16[128,8,2048]{2,1,0:T(8,128)(2,1)}), bf16[128,8,2048]{2,1,0:T(8,128)(2,1)}, u32[]{:S(2)}, u32[]{:S(2)}) async-start(bf16[128,8,2048]{2,1,0:T(8,128)(2,1)} %convert_bitcast_fusion), calls=%async_computation.1 | async-start | bytes 8388608 | tf_op jit(solution)/shard_map/all_to_all | solution.py:288
  197.0 3.1 %copy-start.2 = (bf16[64,2048]{1,0:T(8,128)(2,1)S(1)}, bf16[64,2048]{1,0:T(8,128)(2,1)}, u32[]{:S(2)}) copy-start(bf16[64,2048]{1,0:T(8,128)(2,1)} %get-tuple-element.7) | copy-start | bytes 786436
where the time goes:
time: 201 us
  blocking collectives  58.1 us (29%)
  waiting for transfers between devices  51.5 us (26%)
  Pallas kernels  49.3 us (25%)
  matrix products  22.9 us (11%)
  local copies, waits for them, and re-layouts  8.03 us (4%)
  starting transfers between devices  5.62 us (3%)
  other arithmetic  4.81 us (2%)
    all_to_all x1, blocking collectives, local(): lax.all_to_all(buffer, 'dp', split_axis=0, concat_axis=0, tiled=True)  58.1 us
    all_to_all x1, waiting for transfers between devices, local(): lax.all_to_all(served, 'dp', split_axis=0, concat_axis=0, tiled=True)  51.5 us
    pallas_call x1, Pallas kernels, attention(): pl.pallas_call(attention_kernel, out_shape=[jax.ShapeDtypeStruct((rows, w...  49.3 us
    dot_general x1, matrix products, expert_rows(): jnp.dot(act, down_w[0], preferred_element_type=jnp.float32)  12.2 us
    all_to_all x1, starting transfers between devices, local(): lax.all_to_all(served, 'dp', split_axis=0, concat_axis=0, tiled=True)  5.62 us
    dot_general x1, matrix products, expert_rows(): jnp.dot(flat_rows, gate_w[0], preferred_element_type=jnp.float32)  5.19 us
  transfers between devices with their start and end apart: 1, of which 1 were waited for; matrix products, arithmetic and copies ran while one was open for 1% of the time, Pallas kernels for 0%

commit v1 on v0

--- a/solution.py
+++ b/solution.py
@@ -238,14 +238,125 @@
     )(index, lens, queries, new_kv, residual, gain, q0, q1, pair, prefix, cache, w_out)
 
 
-def expert_rows(block, gate_w, up_w, down_w):
-    block_shape = block.shape
-    flat_rows = block.reshape(-1, block_shape[-1])
-    gate_part = jnp.dot(flat_rows, gate_w[0], preferred_element_type=jnp.float32)
-    up_part = jnp.dot(flat_rows, up_w[0], preferred_element_type=jnp.float32)
-    act = (jax.nn.silu(gate_part) * up_part).astype(jnp.bfloat16)
-    result = jnp.dot(act, down_w[0], preferred_element_type=jnp.float32).astype(jnp.bfloat16)
-    return result.reshape(block_shape)
+def shifted(me, k, i, sign):
+    dx, dy, dc = i % 4, (i // 4) % 4, i // 16
+    dz = (dx + dy + k) % 4
+    z = (me // 32 + 4 + sign * dz) % 4
+    y = ((me // 8) % 4 + 4 + sign * dy) % 4
+    x = ((me // 2) % 4 + 4 + sign * dx) % 4
+    return z * 32 + y * 8 + x * 2 + (me + dc) % 2
+
+
+def experts_kernel(
+    picks_ref, mix_ref, normed_ref, hidden_ref, gate_hbm, up_hbm, down_hbm,
+    out_ref,
+    gate, up, down, outgoing, arrived, served, returned,
+    load_sem, local_sem, send_out, recv_out, send_back, recv_back,
+):
+    me = lax.axis_index("dp")
+    loads = [
+        pltpu.make_async_copy(source.at[0], target, load_sem.at[n])
+        for n, (source, target) in enumerate(((gate_hbm, gate), (up_hbm, up), (down_hbm, down)))
+    ]
+    for copy in loads:
+        copy.start()
+    barrier = pltpu.get_barrier_semaphore()
+    groups, members, capacity, width = outgoing.shape
+    count = members * capacity
+    low = lambda k: 1 if k == 0 else 0
+
+    for k in range(groups):
+        def greet(i, carry, k=k):
+            pl.semaphore_signal(
+                barrier, inc=1, device_id=(shifted(me, k, i, 1),), device_id_type=MESH
+            )
+            return carry
+
+        lax.fori_loop(low(k), members, greet, 0)
+    for k in range(groups):
+        block = dot_n(picks_ref[k * count:(k + 1) * count], normed_ref[...])
+        outgoing[k] = block.astype(jnp.bfloat16).reshape(members, capacity, width)
+    pl.semaphore_wait(barrier, groups * members - 1)
+
+    def transfer(source, target, send_sem, recv_sem, k, part, peer):
+        return pltpu.make_async_remote_copy(
+            src_ref=source.at[k, part], dst_ref=target.at[k, part],
+            send_sem=send_sem.at[k], recv_sem=recv_sem.at[k],
+            device_id=(peer,), device_id_type=MESH,
+        )
+
+    def send(source, target, send_sem, recv_sem, k, sign):
+        def one(i, carry):
+            transfer(
+                source, target, send_sem, recv_sem, k, i, shifted(me, k, i, sign)
+            ).start()
+            return carry
+
+        lax.fori_loop(low(k), members, one, 0)
+
+    def whole(source, target, send_sem, recv_sem, k):
+        part = pl.ds(low(k), members - low(k))
+        return transfer(source, target, send_sem, recv_sem, k, part, shifted(me, k, 1, 1))
+
+    out_args = (outgoing, arrived, send_out, recv_out)
+    back_args = (served, returned, send_back, recv_back)
+    own_out = pltpu.make_async_copy(outgoing.at[0, 0], arrived.at[0, 0], local_sem.at[0])
+    own_back = pltpu.make_async_copy(served.at[0, 0], returned.at[0, 0], local_sem.at[1])
+    own_out.start()
+    for k in range(groups):
+        send(*out_args, k, 1)
+    for copy in loads:
+        copy.wait()
+    own_out.wait()
+    for k in range(groups):
+        whole(*out_args, k).wait_recv()
+        rows = arrived[k].reshape(count, width)
+        gate_part = dot_n(rows, gate[...])
+        act = gate_part / (1.0 + jnp.exp(-gate_part)) * dot_n(rows, up[...])
+        result = dot_n(act.astype(jnp.bfloat16), down[...])
+        served[k] = result.astype(jnp.bfloat16).reshape(members, capacity, width)
+        if k == 0:
+            own_back.start()
+        send(*back_args, k, -1)
+    own_back.wait()
+    total = None
+    for k in range(groups):
+        whole(*back_args, k).wait_recv()
+        part = dot_n(mix_ref[:, k * count:(k + 1) * count], returned[k].reshape(count, width))
+        total = part if total is None else total + part
+    tokens = hidden_ref.shape[0]
+    out_ref[...] = (
+        hidden_ref[...].astype(jnp.float32) + total[:tokens] + total[tokens:]
+    ).astype(jnp.bfloat16)
+    for k in range(groups):
+        whole(*out_args, k).wait_send()
+        whole(*back_args, k).wait_send()
+
+
+def routed_experts(picks, mix, normed, hidden, w_gate, w_up, w_down):
+    tokens, width = hidden.shape
+    vmem = pl.BlockSpec(memory_space=pltpu.VMEM)
+    hbm = pl.BlockSpec(memory_space=pl.ANY)
+    bf16 = jnp.bfloat16
+    dma = pltpu.SemaphoreType.DMA
+    slots = pltpu.VMEM((4, 32, picks.shape[0] // 128, width), bf16)
+    return pl.pallas_call(
+        experts_kernel,
+        out_shape=jax.ShapeDtypeStruct((tokens, width), bf16),
+        in_specs=[vmem] * 4 + [hbm] * 3,
+        out_specs=vmem,
+        scratch_shapes=[
+            pltpu.VMEM(w_gate.shape[1:], bf16),
+            pltpu.VMEM(w_up.shape[1:], bf16),
+            pltpu.VMEM(w_down.shape[1:], bf16),
+            slots, slots, slots, slots,
+            dma((3,)), dma((2,)), dma((4,)), dma((4,)), dma((4,)), dma((4,)),
+        ],
+        compiler_params=pltpu.CompilerParams(
+            collective_id=1, has_side_effects=True, vmem_limit_bytes=56 * 2**20
+        ),
+        name="experts",
+    )(picks, mix, normed, hidden, w_gate, w_up, w_down)
 
 
 def local(
@@ -270,7 +381,8 @@
         index, lens, queries, new_kv, residual, norm_gain.reshape(1, width), q[:, 0], q[:, 1], pair,
         prefix_cache[:, 0], decode_cache, w_out,
     )
-    expert_ids = jnp.arange(experts, dtype=jnp.int32)
+    numbers = jnp.arange(experts, dtype=jnp.int32)
+    expert_ids = shifted(me, numbers // 32, numbers % 32, 1)
     named = routes[:, :, None] == expert_ids[None, None, :]
     member = jnp.any(named, axis=1)
     weight = jnp.sum(jnp.where(named, route_weight[:, :, None], 0.0), axis=1)
@@ -280,22 +392,12 @@
     rank = jnp.where(member, rank, -1.0).T
     slots = jnp.arange(capacity, dtype=jnp.float32)
     chosen = rank[:, None, :] == slots[None, :, None]
-    picks = chosen.reshape(experts * capacity, row_count)
-    buffer = jnp.dot(picks.astype(jnp.bfloat16), normed, preferred_element_type=jnp.float32)
-    buffer = buffer.astype(jnp.bfloat16).reshape(experts, capacity, width)
-    arrived_rows = lax.all_to_all(buffer, "dp", split_axis=0, concat_axis=0, tiled=True)
-    served = expert_rows(arrived_rows, w_gate, w_up, w_down)
-    returned = lax.all_to_all(served, "dp", split_axis=0, concat_axis=0, tiled=True)
-    mix = jnp.where(chosen, weight.T[:, None, :], 0.0).reshape(experts * capacity, row_count)
+    picks = chosen.reshape(experts * capacity, row_count).astype(jnp.bfloat16)
+    mix = jnp.where(chosen, weight.T[:, None, :], 0.0).reshape(experts * capacity, row_count).T
     high = lax.reduce_precision(mix, 8, 7)
     rest = (mix - high).astype(jnp.bfloat16)
-    both = jnp.concatenate([high.astype(jnp.bfloat16), rest], axis=1)
-    sums = lax.dot_general(
-        both, returned.reshape(experts * capacity, width), (((0,), (0,)), ((), ())),
-        preferred_element_type=jnp.float32,
-    )
-    mixed = hidden_state.astype(jnp.float32) + sums[:row_count] + sums[row_count:]
-    return mixed.astype(jnp.bfloat16)
+    both = jnp.concatenate([high.astype(jnp.bfloat16), rest], axis=0)
+    return routed_experts(picks, both, normed, hidden_state, w_gate, w_up, w_down)
 
 
 def solution(mesh):

time: 201 us -> 171 us (0.85); the launches traced: 201 us -> 168 us
  Pallas kernels: 49.3 us -> 154 us
  blocking collectives: 58.1 us -> 0 us
  waiting for transfers between devices: 51.5 us -> 0 us
  matrix products: 22.9 us -> 0.13 us
  starting transfers between devices: 5.62 us -> 0 us
    pallas_call x0 -> x1, Pallas kernels: none -> 104 us  [routed_experts(): pl.pallas_call(experts_kernel, out_shape=jax.ShapeDtypeStruct((tokens, wi...]
    all_to_all x1 -> x0, blocking collectives: 58.1 us -> none  [local(): lax.all_to_all(buffer, 'dp', split_axis=0, concat_axis=0, tiled=True)]
    all_to_all x1 -> x0, waiting for transfers between devices: 51.5 us -> none  [local(): lax.all_to_all(served, 'dp', split_axis=0, concat_axis=0, tiled=True)]
    dot_general x4 -> x0, matrix products: 22.8 us -> none  [the longest x1 12.2 us: expert_rows(): jnp.dot(act, down_w[0], preferred_element_type=jnp.float32)]
    all_to_all x1 -> x0, starting transfers between devices: 5.62 us -> none  [local(): lax.all_to_all(served, 'dp', split_axis=0, concat_axis=0, tiled=True)]
  transfers between devices with their start and end apart: 1 -> 0, of which waited for: 1 -> 0; matrix products, arithmetic and copies ran while one was open for 1% -> 0% of each run, Pallas kernels for 0% -> 0%
where the time goes in v1:
time: 171 us; the launch traced here: 168 us
  Pallas kernels  154 us (90%)
  local copies, waits for them, and re-layouts  9.5 us (6%)
  other arithmetic  4.01 us (2%)
    pallas_call x1, Pallas kernels, routed_experts(): pl.pallas_call(experts_kernel, out_shape=jax.ShapeDtypeStruct((tokens, wi...  104 us
    pallas_call x1, Pallas kernels, attention(): pl.pallas_call(attention_kernel, out_shape=[jax.ShapeDtypeStruct((rows, w...  49.3 us
    unnamed x5, local copies, waits for them, and re-layouts  3.99 us

profile of v1, /device:TPU:1, one launch (start us, length us, event | category | flops | bytes accessed | tf_op | source)
XLA Modules:
  0.0 168.0 jit_solution(4727980294623689709)
XLA Ops:
  0.7 0.8 dynamic_slice.3
  1.5 0.9 select_reduce_fusion
  2.3 0.6 pad_add_fusion.index_ref
  2.9 1.3 pad_add_fusion.1.len_ref
  4.2 0.7 slice.15
  4.9 0.6 copy.37
  5.5 1.3 reshape.162.gain_ref
  6.8 0.8 slice_bitcast_fusion
  7.6 0.6 slice_bitcast_fusion.1
  8.2 0.8 copy.29
  9.0 0.2 compare_reduce_fusion
  9.1 0.1 convolution_select_fusion
  9.3 0.1 copy.30
  9.4 0.8 copy.32
  10.2 0.2 fusion
  10.4 0.1 copy.33
  10.5 0.1 eq.65
  10.6 0.2 copy.34
  10.8 0.2 copy.31
  11.2 0.7 pad_maximum_fusion.mix_ref
  11.9 0.8 copy.38.picks_ref
  12.7 49.3 %attention.1 = (bf16[64,2048]{1,0:T(8,128)(2,1)}, bf16[64,2048]{1,0:T(8,128)(2,1)}) custom-call(s32[8]{0:T(128)} %pad_add_fusion.index_ref, s32[5]{0:T(128)} %pad_add_fusion.1.len_ref, bf16[64,2048]{1,0:T(8,128)(2,1)} %q_ref.1, bf16[2,64,256]{2,1,0:T(8,128)(2,1)} %kv_ref.1, bf16[64,2048]{1,0:T(8,128)(2,1)} %res_ref.1, bf16[1,2048]{1,0:T(2,128)(2,1)} %reshape.162.gain_ref, ...), custom_call_target="tpu_custom_call" | custom-call | tf_op jit(solution)/shard_map/attention/pallas_call | solution.py:213
  62.0 104.3 %experts.1 = bf16[64,2048]{1,0:T(8,128)(2,1)} custom-call(bf16[1024,64]{1,0:T(8,128)(2,1)} %copy.38.picks_ref, bf16[128,1024]{1,0:T(8,128)(2,1)} %pad_maximum_fusion.mix_ref, bf16[64,2048]{1,0:T(8,128)(2,1)} %get-tuple-element.7.normed_ref, bf16[64,2048]{1,0:T(8,128)(2,1)} %get-tuple-element.8.hidden_ref, bf16[1,2048,768]{2,1,0:T(8,128)(2,1)} %gate_hbm.1, ...), custom_call_target="tpu_custom_call" | custom-call | tf_op jit(solution)/shard_map/experts/pallas_call | solution.py:343
  166.4 1.7 copy.46
  (10 shorter events, 0.3 us)

commit v2 on v1

--- a/solution.py
+++ b/solution.py
@@ -86,10 +86,10 @@
 
 
 def attention_kernel(
-    index_ref, len_ref, q_ref, kv_ref, res_ref, gain_ref, q0_ref, q1_ref, pair_ref,
-    prefix_hbm, cache_hbm, wout_hbm,
-    hidden_ref, normed_ref,
-    prefix, cache, wout, att, a0, a1, a2, b0, b1, s0, s1,
+    request_ref, place_ref, len_ref, prior_ref, q_ref, kv_ref, res_ref, gain_ref,
+    routes_ref, weight_ref, prefix_hbm, cache_hbm, wout_hbm,
+    hidden_ref, normed_ref, picks_ref, mix_ref,
+    prefix, cache, wout, att, a0, a1, a2, b0, b1, s0, s1, q0_ref, q1_ref, pair_ref,
     load_sem, send_a, recv_a, local_a, send_b, recv_b, local_b,
 ):
     me = lax.axis_index("dp")
@@ -110,6 +110,16 @@
     pl.semaphore_signal(
         barrier, inc=1, device_id=(me + 1 - 2 * first.core,), device_id_type=MESH
     )
+    last = q_ref[q_ref.shape[0] - 16:, :].astype(jnp.float32)
+    keys = kv_ref[0, kv_ref.shape[1] - 16:, :].astype(jnp.float32)
+    values = kv_ref[1, kv_ref.shape[1] - 16:, :].astype(jnp.float32)
+    for s in range(DEC):
+        row = slice(16 - DEC + s, 17 - DEC + s)
+        for g, target in enumerate((q0_ref, q1_ref)):
+            heads = [last[row, h * HEAD:(h + 1) * HEAD] for h in range(g * GROUP, (g + 1) * GROUP)]
+            target[s] = jnp.concatenate(heads, axis=0).astype(jnp.bfloat16)
+        parts = [plane[row, g * HEAD:(g + 1) * HEAD] for plane in (keys, values) for g in range(2)]
+        pair_ref[s] = jnp.concatenate(parts, axis=0).astype(jnp.bfloat16)
     pl.semaphore_wait(barrier, 10)
     scale = 1.0 / math.sqrt(HEAD)
     rows = q_ref.shape[0]
@@ -123,7 +133,7 @@
         old = dot_t(q, prefix[0, :, cols]) * scale
         new = dot_t(q, kv_ref[0, :, cols]) * scale
         position = lax.broadcasted_iota(jnp.int32, old.shape, 1)
-        old = jnp.where(position < len_ref[DEC], old, MASKED)
+        old = jnp.where(position < prior_ref[0], old, MASKED)
         row = lax.broadcasted_iota(jnp.int32, new.shape, 0) % rows
         new = jnp.where(lax.broadcasted_iota(jnp.int32, new.shape, 1) <= row, new, MASKED)
         top = jnp.maximum(old.max(axis=-1, keepdims=True), new.max(axis=-1, keepdims=True))
@@ -134,22 +144,65 @@
         for j, h in enumerate(heads):
             att[:, h * HEAD:(h + 1) * HEAD] = out[j * rows:(j + 1) * rows]
 
+    def routing():
+        tokens = routes_ref.shape[1]
+        experts = picks_ref.shape[0] // GROUP
+        number = lax.broadcasted_iota(jnp.int32, (experts, tokens), 0)
+        dx, dy, dc = number & 3, (number >> 2) & 3, (number >> 4) & 1
+        dz = (dx + dy + (number >> 5)) & 3
+        expert = (
+            (((me // 32 + dz) & 3) << 5)
+            + ((((me // 8) % 4 + dy) & 3) << 3)
+            + ((((me // 2) % 4 + dx) & 3) << 1)
+            + ((me % 2 + dc) & 1)
+        )
+        member = jnp.zeros((experts, tokens), jnp.float32)
+        weight = jnp.zeros((experts, tokens), jnp.float32)
+        for k in range(routes_ref.shape[0]):
+            named = routes_ref[k:k + 1, :] == expert
+            member = jnp.where(named, 1.0, member)
+            weight = jnp.where(named, weight_ref[k:k + 1, :], weight)
+        one = lax.broadcasted_iota(jnp.int32, (tokens, tokens), 0)
+        two = lax.broadcasted_iota(jnp.int32, (tokens, tokens), 1)
+        earlier = jnp.where(one < two, 1.0, 0.0).astype(jnp.bfloat16)
+        same = jnp.where(one == two, 1.0, 0.0).astype(jnp.bfloat16)
+        rank = dot_n(member.astype(jnp.bfloat16), earlier)
+        rank = jnp.where(member > 0.5, rank, -1.0).astype(jnp.bfloat16)
+        high = weight.astype(jnp.bfloat16)
+        rest = (weight - high.astype(jnp.float32)).astype(jnp.bfloat16)
+        slots = picks_ref.shape[0]
+        down = lax.broadcasted_iota(jnp.int32, (slots, experts), 0) >> 3
+        spread = jnp.where(
+            down == lax.broadcasted_iota(jnp.int32, (slots, experts), 1), 1.0, 0.0
+        ).astype(jnp.bfloat16)
+        wanted = (lax.broadcasted_iota(jnp.int32, (slots, tokens), 0) & 7).astype(jnp.float32)
+        picks_ref[...] = jnp.where(dot_n(spread, rank) == wanted, 1.0, 0.0).astype(jnp.bfloat16)
+        wanted = (lax.broadcasted_iota(jnp.int32, (tokens, slots), 1) & 7).astype(jnp.float32)
+        turned = dot_t(same, rank).astype(jnp.bfloat16)
+        chosen = dot_t(turned, spread) == wanted
+        for n, table in enumerate((high, rest)):
+            turned = dot_t(same, table).astype(jnp.bfloat16)
+            mix_ref[n * tokens:(n + 1) * tokens, :] = jnp.where(
+                chosen, dot_t(turned, spread), 0.0
+            ).astype(jnp.bfloat16)
+
     first.start(0)
+    first.finish()
+    first.start(1)
     loads[0].wait()
     prefill(0)
     first.finish()
-    first.start(1)
+    first.start(2)
     prefill(1)
-    first.finish()
-    first.start(2)
     prefill(2)
     first.finish()
     first.start(3)
     loads[1].wait()
+    routing()
     first.finish()
 
     for s in range(DEC):
-        src = index_ref[s]
+        src = request_ref[s]
         sz, sy, sx, sc = src // 128, (src // 32) % 4, (src // 8) % 4, (src // 4) % 2
         sr = src % 4
         pair = a2[sz, sy, sx, sc, sr].astype(jnp.float32)
@@ -168,17 +221,17 @@
             out_ref[s] = (out + own * pair[2 + g:3 + g]).astype(jnp.bfloat16)
 
     second.start(0)
-    prefill(3)
     second.finish()
     second.start(1)
-    loads[2].wait()
     second.finish()
     second.start(2)
+    prefill(3)
+    loads[2].wait()
     second.finish()
     second.start(3)
     second.finish()
     for s in range(DEC):
-        src = index_ref[DEC + s]
+        src = place_ref[me * DEC + s]
         sz, sy, sx, sc = src // 128, (src // 32) % 4, (src // 8) % 4, (src // 4) % 2
         sr = src % 4
         for g, buf in enumerate((b0, b1)):
@@ -198,13 +251,20 @@
         piece = piece.astype(jnp.float32)
         total += (piece * piece).sum(axis=-1, keepdims=True)
     norm = lax.rsqrt(total * (1.0 / width) + EPSILON)
-    normed_ref[...] = (
-        hidden_ref[...].astype(jnp.float32) * norm * gain_ref[...].astype(jnp.float32)
-    ).astype(jnp.bfloat16)
-
-
-def attention(index, lens, queries, new_kv, residual, gain, q0, q1, pair, prefix, cache, w_out):
+    gain = gain_ref[...].astype(jnp.float32)
+    for n in range(width // HEAD):
+        cols = slice(n * HEAD, (n + 1) * HEAD)
+        piece = hidden_ref[:, cols].astype(jnp.float32) * norm * gain[n:n + 1]
+        normed_ref[:, cols] = piece.astype(jnp.bfloat16)
+
+
+def attention(
+    request, placement, cache_len, prefix_len, queries, new_kv, residual, gain, routes, weights,
+    prefix, cache, w_out,
+):
     rows, width = residual.shape
+    slots = lax.axis_size("dp") * GROUP
+    quarter, pair = (DEC, GROUP, HEAD), (DEC, 4, HEAD)
     vmem = pl.BlockSpec(memory_space=pltpu.VMEM)
     smem = pl.BlockSpec(memory_space=pltpu.SMEM)
     hbm = pl.BlockSpec(memory_space=pl.ANY)
@@ -212,21 +272,29 @@
     dma = pltpu.SemaphoreType.DMA
     return pl.pallas_call(
         attention_kernel,
-        out_shape=[jax.ShapeDtypeStruct((rows, width), bf16)] * 2,
-        in_specs=[smem, smem] + [vmem] * 7 + [hbm] * 3,
-        out_specs=[vmem, vmem],
+        out_shape=[
+            jax.ShapeDtypeStruct((rows, width), bf16),
+            jax.ShapeDtypeStruct((rows, width), bf16),
+            jax.ShapeDtypeStruct((slots, rows), bf16),
+            jax.ShapeDtypeStruct((2 * rows, slots), bf16),
+        ],
+        in_specs=[smem] * 4 + [vmem] * 6 + [hbm] * 3,
+        out_specs=[vmem] * 4,
         scratch_shapes=[
             pltpu.VMEM(prefix.shape, bf16),
             pltpu.VMEM(cache.shape, bf16),
             pltpu.VMEM(w_out.shape, bf16),
             pltpu.VMEM((rows, queries.shape[1]), jnp.float32),
-            pltpu.VMEM((4, 4, 4, 2) + q0.shape, bf16),
-            pltpu.VMEM((4, 4, 4, 2) + q1.shape, bf16),
-            pltpu.VMEM((4, 4, 4, 2) + pair.shape, bf16),
-            pltpu.VMEM((4, 4, 4, 2) + q0.shape, bf16),
-            pltpu.VMEM((4, 4, 4, 2) + q1.shape, bf16),
-            pltpu.VMEM(q0.shape, bf16),
-            pltpu.VMEM(q1.shape, bf16),
+            pltpu.VMEM((4, 4, 4, 2) + quarter, bf16),
+            pltpu.VMEM((4, 4, 4, 2) + quarter, bf16),
+            pltpu.VMEM((4, 4, 4, 2) + pair, bf16),
+            pltpu.VMEM((4, 4, 4, 2) + quarter, bf16),
+            pltpu.VMEM((4, 4, 4, 2) + quarter, bf16),
+            pltpu.VMEM(quarter, bf16),
+            pltpu.VMEM(quarter, bf16),
+            pltpu.VMEM(quarter, bf16),
+            pltpu.VMEM(quarter, bf16),
+            pltpu.VMEM(pair, bf16),
             dma((3,)),
             dma((3, 10)), dma((3, 10)), dma((3,)),
             dma((2, 10)), dma((2, 10)), dma((2,)),
@@ -235,7 +303,10 @@
             collective_id=0, has_side_effects=True, vmem_limit_bytes=56 * 2**20
         ),
         name="attention",
-    )(index, lens, queries, new_kv, residual, gain, q0, q1, pair, prefix, cache, w_out)
+    )(
+        request, placement, cache_len, prefix_len, queries, new_kv, residual, gain, routes, weights,
+        prefix, cache, w_out,
+    )
 
 
 def shifted(me, k, i, sign):
@@ -248,7 +319,7 @@
 
 
 def experts_kernel(
-    picks_ref, mix_ref, normed_ref, hidden_ref, gate_hbm, up_hbm, down_hbm,
+    picks_ref, mix_ref, normed_ref, gate_hbm, up_hbm, down_hbm,
     out_ref,
     gate, up, down, outgoing, arrived, served, returned,
     load_sem, local_sem, send_out, recv_out, send_back, recv_back,
@@ -324,17 +395,15 @@
         whole(*back_args, k).wait_recv()
         part = dot_n(mix_ref[:, k * count:(k + 1) * count], returned[k].reshape(count, width))
         total = part if total is None else total + part
-    tokens = hidden_ref.shape[0]
-    out_ref[...] = (
-        hidden_ref[...].astype(jnp.float32) + total[:tokens] + total[tokens:]
-    ).astype(jnp.bfloat16)
+    tokens = out_ref.shape[0]
+    out_ref[...] = total[:tokens] + total[tokens:]
     for k in range(groups):
         whole(*out_args, k).wait_send()
         whole(*back_args, k).wait_send()
 
 
-def routed_experts(picks, mix, normed, hidden, w_gate, w_up, w_down):
-    tokens, width = hidden.shape
+def routed_experts(picks, mix, normed, w_gate, w_up, w_down):
+    tokens, width = normed.shape
     vmem = pl.BlockSpec(memory_space=pltpu.VMEM)
     hbm = pl.BlockSpec(memory_space=pl.ANY)
     bf16 = jnp.bfloat16
@@ -342,8 +411,8 @@
     slots = pltpu.VMEM((4, 32, picks.shape[0] // 128, width), bf16)
     return pl.pallas_call(
         experts_kernel,
-        out_shape=jax.ShapeDtypeStruct((tokens, width), bf16),
-        in_specs=[vmem] * 4 + [hbm] * 3,
+        out_shape=jax.ShapeDtypeStruct((tokens, width), jnp.float32),
+        in_specs=[vmem] * 3 + [hbm] * 3,
         out_specs=vmem,
         scratch_shapes=[
             pltpu.VMEM(w_gate.shape[1:], bf16),
@@ -356,48 +425,26 @@
             collective_id=1, has_side_effects=True, vmem_limit_bytes=56 * 2**20
         ),
         name="experts",
-    )(picks, mix, normed, hidden, w_gate, w_up, w_down)
+    )(picks, mix, normed, w_gate, w_up, w_down)
 
 
 def local(
     queries, new_kv, residual, prefix_cache, prefix_len, decode_cache, cache_len, placement,
     w_out, norm_gain, routes, route_weight, w_gate, w_up, w_down,
 ):
-    row_count, width = residual.shape
-    experts = lax.axis_size("dp")
-    capacity = max(2, 2 * row_count * routes.shape[1] // experts)
+    width = residual.shape[1]
     me = lax.axis_index("dp")
     slot_ids = me * DEC + jnp.arange(DEC, dtype=jnp.int32)
     request_ids = jnp.arange(placement.shape[0], dtype=jnp.int32)
     matches = placement[None, :] == slot_ids[:, None]
     request = jnp.sum(jnp.where(matches, request_ids[None, :], 0), axis=1)
-    my_slots = lax.dynamic_slice_in_dim(placement, me * DEC, DEC)
-    index = jnp.concatenate([request, my_slots])
-    lens = jnp.concatenate([cache_len, prefix_len])
-    q = queries[STRETCH:].reshape(DEC, 2, GROUP, HEAD)
-    pair = jnp.transpose(new_kv[:, STRETCH:].reshape(2, DEC, 2, HEAD), (1, 0, 2, 3))
-    pair = pair.reshape(DEC, 4, HEAD)
-    hidden_state, normed = attention(
-        index, lens, queries, new_kv, residual, norm_gain.reshape(1, width), q[:, 0], q[:, 1], pair,
+    hidden_state, normed, picks, mix = attention(
+        request, placement, cache_len, prefix_len, queries, new_kv, residual,
+        norm_gain.reshape(width // HEAD, HEAD), routes.T, route_weight.T,
         prefix_cache[:, 0], decode_cache, w_out,
     )
-    numbers = jnp.arange(experts, dtype=jnp.int32)
-    expert_ids = shifted(me, numbers // 32, numbers % 32, 1)
-    named = routes[:, :, None] == expert_ids[None, None, :]
-    member = jnp.any(named, axis=1)
-    weight = jnp.sum(jnp.where(named, route_weight[:, :, None], 0.0), axis=1)
-    row_ids = jnp.arange(row_count, dtype=jnp.int32)
-    lower = (row_ids[None, :] < row_ids[:, None]).astype(jnp.bfloat16)
-    rank = jnp.dot(lower, member.astype(jnp.bfloat16), preferred_element_type=jnp.float32)
-    rank = jnp.where(member, rank, -1.0).T
-    slots = jnp.arange(capacity, dtype=jnp.float32)
-    chosen = rank[:, None, :] == slots[None, :, None]
-    picks = chosen.reshape(experts * capacity, row_count).astype(jnp.bfloat16)
-    mix = jnp.where(chosen, weight.T[:, None, :], 0.0).reshape(experts * capacity, row_count).T
-    high = lax.reduce_precision(mix, 8, 7)
-    rest = (mix - high).astype(jnp.bfloat16)
-    both = jnp.concatenate([high.astype(jnp.bfloat16), rest], axis=0)
-    return routed_experts(picks, both, normed, hidden_state, w_gate, w_up, w_down)
+    expert_sum = routed_experts(picks, mix, normed, w_gate, w_up, w_down)
+    return (hidden_state.astype(jnp.float32) + expert_sum).astype(jnp.bfloat16)
 
 
 def solution(mesh):

time: 171 us -> 161 us (0.942)
  local copies, waits for them, and re-layouts: 9.5 us -> 0.01 us
    unnamed x5 -> x2, local copies, waits for them, and re-layouts: 3.99 us -> 0.01 us
    concatenate x3 -> x0, other arithmetic: 2.61 us -> none  [the longest x1 1.29 us: local(): lens = jnp.concatenate([cache_len, prefix_len])]
    reshape x3 -> x0, local copies, waits for them, and re-layouts: 1.88 us -> none  [the longest x1 1.28 us: local(): norm_gain.reshape(1, width)]
where the time goes in v2:
time: 161 us; the launch traced here: 158 us
  Pallas kernels  154 us (96%)
  other arithmetic  3.17 us (2%)
    pallas_call x1, Pallas kernels, routed_experts(): pl.pallas_call(experts_kernel, out_shape=jax.ShapeDtypeStruct((tokens, wi...  104 us
    pallas_call x1, Pallas kernels, attention(): pl.pallas_call(attention_kernel, out_shape=[jax.ShapeDtypeStruct((rows, w...  49.4 us

profile of v2, /device:TPU:1, one launch (start us, length us, event | category | flops | bytes accessed | tf_op | source)
XLA Modules:
  0.0 157.6 jit_solution(7929663242698088905)
XLA Ops:
  0.7 1.4 select_reduce_fusion.request_ref
  2.0 49.4 %attention.1 = (bf16[64,2048]{1,0:T(8,128)(2,1)}, bf16[64,2048]{1,0:T(8,128)(2,1)}, bf16[1024,64]{1,0:T(8,128)(2,1)}, bf16[128,1024]{1,0:T(8,128)(2,1)}) custom-call(s32[4]{0:T(128)} %select_reduce_fusion.request_ref, s32[512]{0:T(512)} %place_ref.1, s32[4]{0:T(128)} %len_ref.1, s32[1]{0:T(128)S(6)} %copy.16.prior_ref, bf16[64,2048]{1,0:T(8,128)(2,1)} %q_ref.1, ...), custom_call_target="tpu_custom_call" | custom-call | tf_op jit(solution)/shard_map/attention/pallas_call | solution.py:273
  51.4 0.0 copy-start
  51.4 104.3 %experts.1 = f32[64,2048]{1,0:T(8,128)} custom-call(bf16[1024,64]{1,0:T(8,128)(2,1)} %get-tuple-element.10.picks_ref, bf16[128,1024]{1,0:T(8,128)(2,1)} %get-tuple-element.11.mix_ref, bf16[64,2048]{1,0:T(8,128)(2,1)} %get-tuple-element.12.normed_ref, bf16[1,2048,768]{2,1,0:T(8,128)(2,1)} %gate_hbm.1, bf16[1,2048,768]{2,1,0:T(8,128)(2,1)} %up_hbm.1, ...), custom_call_target="tpu_custom_call" | custom-call | tf_op jit(solution)/shard_map/experts/pallas_call | solution.py:412
  155.8 0.0 copy-done
  155.8 1.8 %add_convert_fusion = bf16[64,2048]{1,0:T(8,128)(2,1)} fusion(f32[64,2048]{1,0:T(8,128)} %experts.1, bf16[64,2048]{1,0:T(8,128)(2,1)S(1)} %copy-done), kind=kLoop, calls=%fused_computation | loop fusion | flops 393216 | bytes 1048576 | tf_op jit(solution)/shard_map/convert_element_type | solution.py:447
  (1 shorter events, 0.0 us)
Async XLA Ops:
  51.4 104.4 %copy-start = (bf16[64,2048]{1,0:T(8,128)(2,1)S(1)}, bf16[64,2048]{1,0:T(8,128)(2,1)}, u32[]{:S(2)}) copy-start(bf16[64,2048]{1,0:T(8,128)(2,1)} %get-tuple-element.9) | copy-start | bytes 786436

commit v3 on v2

--- a/solution.py
+++ b/solution.py
@@ -1,4 +1,3 @@
-import functools
 import math
 
 import jax
@@ -50,29 +49,16 @@
                 own = pltpu.make_async_copy(source, self.slot(buffer, ()), self.local_sem.at[p])
                 own.start()
                 started.append(own)
-            if phase < 3:
-                here = self.slot(buffer, order[:phase])
-                axis = order[phase]
-                for d in range(1, 4):
-                    peer = self.me + ((self.coords[axis] + d) % 4 - self.coords[axis]) * STRIDES[axis]
-                    copy = pltpu.make_async_remote_copy(
-                        src_ref=source if phase == 0 else here,
-                        dst_ref=here,
-                        send_sem=self.send_sem.at[p, phase * 3 + d - 1],
-                        recv_sem=self.recv_sem.at[p, phase * 3 + d - 1],
-                        device_id=(peer,),
-                        device_id_type=MESH,
-                    )
-                    copy.start()
-                    started.append(copy)
-            else:
-                here = self.slot(buffer, (0, 1, 2))
+            here = self.slot(buffer, order[:phase])
+            axis = order[phase]
+            for d in range(1, 4):
+                peer = self.me + ((self.coords[axis] + d) % 4 - self.coords[axis]) * STRIDES[axis]
                 copy = pltpu.make_async_remote_copy(
-                    src_ref=here,
+                    src_ref=source if phase == 0 else here,
                     dst_ref=here,
-                    send_sem=self.send_sem.at[p, 9],
-                    recv_sem=self.recv_sem.at[p, 9],
-                    device_id=(self.me + 1 - 2 * self.core,),
+                    send_sem=self.send_sem.at[p, phase * 3 + d - 1],
+                    recv_sem=self.recv_sem.at[p, phase * 3 + d - 1],
+                    device_id=(peer,),
                     device_id_type=MESH,
                 )
                 copy.start()
@@ -84,13 +70,46 @@
             copy.wait()
         self.started = []
 
-
-def attention_kernel(
+    def forward(self, p, d):
+        axis = ORDERS[p][2]
+        index = [slice(None)] * 3
+        index[axis] = (self.coords[axis] + 4 - d) % 4
+        block = self.buffers[p].at[tuple(index) + (self.core,)]
+        copy = pltpu.make_async_remote_copy(
+            src_ref=block,
+            dst_ref=block,
+            send_sem=self.send_sem.at[p, 9 + d],
+            recv_sem=self.recv_sem.at[p, 9 + d],
+            device_id=(self.me + 1 - 2 * self.core,),
+            device_id_type=MESH,
+        )
+        copy.start()
+        return copy
+
+    def start_last(self):
+        self.start(2)
+        self.passed = [self.forward(p, 0) for p in range(len(self.buffers))]
+
+    def finish_last(self):
+        for d in (1, 3, 2):
+            for p in range(len(self.buffers)):
+                self.started[p * 3 + d - 1].wait_recv()
+                self.passed.append(self.forward(p, d))
+        for copy in self.started:
+            copy.wait_send()
+        for copy in self.passed:
+            copy.wait()
+        self.started = []
+
+
+def layer_kernel(
     request_ref, place_ref, len_ref, prior_ref, q_ref, kv_ref, res_ref, gain_ref,
-    routes_ref, weight_ref, prefix_hbm, cache_hbm, wout_hbm,
+    routes_ref, weight_ref, prefix_hbm, cache_hbm, wout_hbm, gate_hbm, up_hbm, down_hbm,
+    out_ref,
     hidden_ref, normed_ref, picks_ref, mix_ref,
-    prefix, cache, wout, att, a0, a1, a2, b0, b1, s0, s1, q0_ref, q1_ref, pair_ref,
+    prefix, cache, wout, att, a0, a1, a2, b0, b1, b2, s0, s1, s2, q0_ref, q1_ref, pair_ref,
     load_sem, send_a, recv_a, local_a, send_b, recv_b, local_b,
+    *expert_refs,
 ):
     me = lax.axis_index("dp")
     loads = [
@@ -98,10 +117,14 @@
         pltpu.make_async_copy(cache_hbm, cache, load_sem.at[1]),
         pltpu.make_async_copy(wout_hbm, wout, load_sem.at[2]),
     ]
+    loads += [
+        pltpu.make_async_copy(source.at[0], target, load_sem.at[3 + n])
+        for n, (source, target) in enumerate(zip((gate_hbm, up_hbm, down_hbm), expert_refs[:3]))
+    ]
     for copy in loads:
         copy.start()
     first = Gather(me, (q0_ref, q1_ref, pair_ref), (a0, a1, a2), send_a, recv_a, local_a)
-    second = Gather(me, (s0, s1), (b0, b1), send_b, recv_b, local_b)
+    second = Gather(me, (s0, s1, s2), (b0, b1, b2), send_b, recv_b, local_b)
     barrier = pltpu.get_barrier_semaphore()
     for axis in range(3):
         for d in range(1, 4):
@@ -192,21 +215,18 @@
     loads[0].wait()
     prefill(0)
     first.finish()
-    first.start(2)
+    first.start_last()
     prefill(1)
     prefill(2)
-    first.finish()
-    first.start(3)
     loads[1].wait()
-    routing()
-    first.finish()
+    first.finish_last()
 
     for s in range(DEC):
         src = request_ref[s]
         sz, sy, sx, sc = src // 128, (src // 32) % 4, (src // 8) % 4, (src // 4) % 2
         sr = src % 4
         pair = a2[sz, sy, sx, sc, sr].astype(jnp.float32)
-        for g, (buf, out_ref) in enumerate(((a0, s0), (a1, s1))):
+        for g, (buf, target) in enumerate(((a0, s0), (a1, s1))):
             q = buf[sz, sy, sx, sc, sr]
             cols = slice(g * HEAD, (g + 1) * HEAD)
             old = dot_t(q, cache[0, s, :, cols]) * scale
@@ -218,24 +238,28 @@
             inv = 1.0 / (old.sum(axis=-1, keepdims=True) + new)
             out = dot_n((old * inv).astype(jnp.bfloat16), cache[1, s, :, cols])
             own = (new * inv).astype(jnp.bfloat16).astype(jnp.float32)
-            out_ref[s] = (out + own * pair[2 + g:3 + g]).astype(jnp.bfloat16)
+            result = (out + own * pair[2 + g:3 + g]).astype(jnp.bfloat16)
+            if s < DEC - 1:
+                target[s] = result
+            else:
+                s2[g] = result
 
     second.start(0)
     second.finish()
     second.start(1)
+    prefill(3)
     second.finish()
-    second.start(2)
-    prefill(3)
+    second.start_last()
+    routing()
     loads[2].wait()
-    second.finish()
-    second.start(3)
-    second.finish()
+    second.finish_last()
     for s in range(DEC):
         src = place_ref[me * DEC + s]
         sz, sy, sx, sc = src // 128, (src // 32) % 4, (src // 8) % 4, (src // 4) % 2
         sr = src % 4
         for g, buf in enumerate((b0, b1)):
-            out = buf[sz, sy, sx, sc, sr].astype(jnp.float32)
+            out = buf[sz, sy, sx, sc, jnp.minimum(sr, DEC - 2)].astype(jnp.float32)
+            out = jnp.where(sr < DEC - 1, out, b2[sz, sy, sx, sc, g].astype(jnp.float32))
             for j in range(GROUP):
                 h = g * GROUP + j
                 att[STRETCH + s:STRETCH + s + 1, h * HEAD:(h + 1) * HEAD] = out[j:j + 1]
@@ -257,56 +281,10 @@
         piece = hidden_ref[:, cols].astype(jnp.float32) * norm * gain[n:n + 1]
         normed_ref[:, cols] = piece.astype(jnp.bfloat16)
 
-
-def attention(
-    request, placement, cache_len, prefix_len, queries, new_kv, residual, gain, routes, weights,
-    prefix, cache, w_out,
-):
-    rows, width = residual.shape
-    slots = lax.axis_size("dp") * GROUP
-    quarter, pair = (DEC, GROUP, HEAD), (DEC, 4, HEAD)
-    vmem = pl.BlockSpec(memory_space=pltpu.VMEM)
-    smem = pl.BlockSpec(memory_space=pltpu.SMEM)
-    hbm = pl.BlockSpec(memory_space=pl.ANY)
-    bf16 = jnp.bfloat16
-    dma = pltpu.SemaphoreType.DMA
-    return pl.pallas_call(
-        attention_kernel,
-        out_shape=[
-            jax.ShapeDtypeStruct((rows, width), bf16),
-            jax.ShapeDtypeStruct((rows, width), bf16),
-            jax.ShapeDtypeStruct((slots, rows), bf16),
-            jax.ShapeDtypeStruct((2 * rows, slots), bf16),
-        ],
-        in_specs=[smem] * 4 + [vmem] * 6 + [hbm] * 3,
-        out_specs=[vmem] * 4,
-        scratch_shapes=[
-            pltpu.VMEM(prefix.shape, bf16),
-            pltpu.VMEM(cache.shape, bf16),
-            pltpu.VMEM(w_out.shape, bf16),
-            pltpu.VMEM((rows, queries.shape[1]), jnp.float32),
-            pltpu.VMEM((4, 4, 4, 2) + quarter, bf16),
-            pltpu.VMEM((4, 4, 4, 2) + quarter, bf16),
-            pltpu.VMEM((4, 4, 4, 2) + pair, bf16),
-            pltpu.VMEM((4, 4, 4, 2) + quarter, bf16),
-            pltpu.VMEM((4, 4, 4, 2) + quarter, bf16),
-            pltpu.VMEM(quarter, bf16),
-            pltpu.VMEM(quarter, bf16),
-            pltpu.VMEM(quarter, bf16),
-            pltpu.VMEM(quarter, bf16),
-            pltpu.VMEM(pair, bf16),
-            dma((3,)),
-            dma((3, 10)), dma((3, 10)), dma((3,)),
-            dma((2, 10)), dma((2, 10)), dma((2,)),
-        ],
-        compiler_params=pltpu.CompilerParams(
-            collective_id=0, has_side_effects=True, vmem_limit_bytes=56 * 2**20
-        ),
-        name="attention",
-    )(
-        request, placement, cache_len, prefix_len, queries, new_kv, residual, gain, routes, weights,
-        prefix, cache, w_out,
-    )
+    total = experts_stage(me, picks_ref, mix_ref, normed_ref, loads[3:], *expert_refs)
+    out_ref[...] = (
+        hidden_ref[...].astype(jnp.float32) + total[:rows] + total[rows:]
+    ).astype(jnp.bfloat16)
 
 
 def shifted(me, k, i, sign):
@@ -318,36 +296,14 @@
     return z * 32 + y * 8 + x * 2 + (me + dc) % 2
 
 
-def experts_kernel(
-    picks_ref, mix_ref, normed_ref, gate_hbm, up_hbm, down_hbm,
-    out_ref,
+def experts_stage(
+    me, picks_ref, mix_ref, normed_ref, loads,
     gate, up, down, outgoing, arrived, served, returned,
-    load_sem, local_sem, send_out, recv_out, send_back, recv_back,
+    local_sem, send_out, recv_out, send_back, recv_back,
 ):
-    me = lax.axis_index("dp")
-    loads = [
-        pltpu.make_async_copy(source.at[0], target, load_sem.at[n])
-        for n, (source, target) in enumerate(((gate_hbm, gate), (up_hbm, up), (down_hbm, down)))
-    ]
-    for copy in loads:
-        copy.start()
-    barrier = pltpu.get_barrier_semaphore()
     groups, members, capacity, width = outgoing.shape
     count = members * capacity
     low = lambda k: 1 if k == 0 else 0
-
-    for k in range(groups):
-        def greet(i, carry, k=k):
-            pl.semaphore_signal(
-                barrier, inc=1, device_id=(shifted(me, k, i, 1),), device_id_type=MESH
-            )
-            return carry
-
-        lax.fori_loop(low(k), members, greet, 0)
-    for k in range(groups):
-        block = dot_n(picks_ref[k * count:(k + 1) * count], normed_ref[...])
-        outgoing[k] = block.astype(jnp.bfloat16).reshape(members, capacity, width)
-    pl.semaphore_wait(barrier, groups * members - 1)
 
     def transfer(source, target, send_sem, recv_sem, k, part, peer):
         return pltpu.make_async_remote_copy(
@@ -373,9 +329,14 @@
     back_args = (served, returned, send_back, recv_back)
     own_out = pltpu.make_async_copy(outgoing.at[0, 0], arrived.at[0, 0], local_sem.at[0])
     own_back = pltpu.make_async_copy(served.at[0, 0], returned.at[0, 0], local_sem.at[1])
-    own_out.start()
     for k in range(groups):
-        send(*out_args, k, 1)
+        block = dot_n(picks_ref[k * count:(k + 1) * count], normed_ref[...])
+        outgoing[k] = block.astype(jnp.bfloat16).reshape(members, capacity, width)
+        if k == 1:
+            own_out.start()
+        if k:
+            send(*out_args, k - 1, 1)
+    send(*out_args, groups - 1, 1)
     for copy in loads:
         copy.wait()
     own_out.wait()
@@ -395,37 +356,68 @@
         whole(*back_args, k).wait_recv()
         part = dot_n(mix_ref[:, k * count:(k + 1) * count], returned[k].reshape(count, width))
         total = part if total is None else total + part
-    tokens = out_ref.shape[0]
-    out_ref[...] = total[:tokens] + total[tokens:]
     for k in range(groups):
         whole(*out_args, k).wait_send()
         whole(*back_args, k).wait_send()
-
-
-def routed_experts(picks, mix, normed, w_gate, w_up, w_down):
-    tokens, width = normed.shape
+    return total
+
+
+def layer(
+    request, placement, cache_len, prefix_len, queries, new_kv, residual, gain, routes, weights,
+    prefix, cache, w_out, w_gate, w_up, w_down,
+):
+    rows, width = residual.shape
+    slots = lax.axis_size("dp") * GROUP
+    quarter, pair = (DEC, GROUP, HEAD), (DEC, 4, HEAD)
     vmem = pl.BlockSpec(memory_space=pltpu.VMEM)
+    smem = pl.BlockSpec(memory_space=pltpu.SMEM)
     hbm = pl.BlockSpec(memory_space=pl.ANY)
     bf16 = jnp.bfloat16
     dma = pltpu.SemaphoreType.DMA
-    slots = pltpu.VMEM((4, 32, picks.shape[0] // 128, width), bf16)
+    lane = pltpu.VMEM((4, slots // (4 * GROUP), GROUP, width), bf16)
     return pl.pallas_call(
-        experts_kernel,
-        out_shape=jax.ShapeDtypeStruct((tokens, width), jnp.float32),
-        in_specs=[vmem] * 3 + [hbm] * 3,
+        layer_kernel,
+        out_shape=jax.ShapeDtypeStruct((rows, width), bf16),
+        in_specs=[smem] * 4 + [vmem] * 6 + [hbm] * 6,
         out_specs=vmem,
         scratch_shapes=[
+            pltpu.VMEM((rows, width), bf16),
+            pltpu.VMEM((rows, width), bf16),
+            pltpu.VMEM((slots, rows), bf16),
+            pltpu.VMEM((2 * rows, slots), bf16),
+            pltpu.VMEM(prefix.shape, bf16),
+            pltpu.VMEM(cache.shape, bf16),
+            pltpu.VMEM(w_out.shape, bf16),
+            pltpu.VMEM((rows, queries.shape[1]), jnp.float32),
+            pltpu.VMEM((4, 4, 4, 2) + quarter, bf16),
+            pltpu.VMEM((4, 4, 4, 2) + quarter, bf16),
+            pltpu.VMEM((4, 4, 4, 2) + pair, bf16),
+            pltpu.VMEM((4, 4, 4, 2) + (3, GROUP, HEAD), bf16),
+            pltpu.VMEM((4, 4, 4, 2) + (3, GROUP, HEAD), bf16),
+            pltpu.VMEM((4, 4, 4, 2) + (2, GROUP, HEAD), bf16),
+            pltpu.VMEM((3, GROUP, HEAD), bf16),
+            pltpu.VMEM((3, GROUP, HEAD), bf16),
+            pltpu.VMEM((2, GROUP, HEAD), bf16),
+            pltpu.VMEM(quarter, bf16),
+            pltpu.VMEM(quarter, bf16),
+            pltpu.VMEM(pair, bf16),
+            dma((6,)),
+            dma((3, 13)), dma((3, 13)), dma((3,)),
+            dma((3, 13)), dma((3, 13)), dma((3,)),
             pltpu.VMEM(w_gate.shape[1:], bf16),
             pltpu.VMEM(w_up.shape[1:], bf16),
             pltpu.VMEM(w_down.shape[1:], bf16),
-            slots, slots, slots, slots,
-            dma((3,)), dma((2,)), dma((4,)), dma((4,)), dma((4,)), dma((4,)),
+            lane, lane, lane, lane,
+            dma((2,)), dma((4,)), dma((4,)), dma((4,)), dma((4,)),
         ],
         compiler_params=pltpu.CompilerParams(
-            collective_id=1, has_side_effects=True, vmem_limit_bytes=56 * 2**20
+            collective_id=0, has_side_effects=True, vmem_limit_bytes=60 * 2**20
         ),
-        name="experts",
-    )(picks, mix, normed, w_gate, w_up, w_down)
+        name="layer",
+    )(
+        request, placement, cache_len, prefix_len, queries, new_kv, residual, gain, routes, weights,
+        prefix, cache, w_out, w_gate, w_up, w_down,
+    )
 
 
 def local(
@@ -438,13 +430,11 @@
     request_ids = jnp.arange(placement.shape[0], dtype=jnp.int32)
     matches = placement[None, :] == slot_ids[:, None]
     request = jnp.sum(jnp.where(matches, request_ids[None, :], 0), axis=1)
-    hidden_state, normed, picks, mix = attention(
+    return layer(
         request, placement, cache_len, prefix_len, queries, new_kv, residual,
         norm_gain.reshape(width // HEAD, HEAD), routes.T, route_weight.T,
-        prefix_cache[:, 0], decode_cache, w_out,
+        prefix_cache[:, 0], decode_cache, w_out, w_gate, w_up, w_down,
     )
-    expert_sum = routed_experts(picks, mix, normed, w_gate, w_up, w_down)
-    return (hidden_state.astype(jnp.float32) + expert_sum).astype(jnp.bfloat16)
 
 
 def solution(mesh):

time: 161 us -> 155 us (0.963)
  the two profiles are of different devices: /device:TPU:1 before, /device:TPU:13 now
where the time goes in v3:
time: 155 us
  Pallas kernels  152 us (98%)
  local copies, waits for them, and re-layouts  1.67 us (1%)
    pallas_call x1, Pallas kernels, layer(): pl.pallas_call(layer_kernel, out_shape=jax.ShapeDtypeStruct((rows, width)...  152 us

profile of v3, /device:TPU:13, one launch (start us, length us, event | category | flops | bytes accessed | tf_op | source)
XLA Modules:
  0.0 155.2 jit_solution(14194590950603346359)
XLA Ops:
  0.7 1.4 select_reduce_fusion.request_ref
  2.0 151.5 %layer.1 = bf16[64,2048]{1,0:T(8,128)(2,1)} custom-call(s32[4]{0:T(128)} %select_reduce_fusion.request_ref, s32[512]{0:T(512)} %place_ref.1, s32[4]{0:T(128)} %len_ref.1, s32[1]{0:T(128)S(6)} %copy.17.prior_ref, bf16[64,2048]{1,0:T(8,128)(2,1)} %q_ref.1, bf16[2,64,256]{2,1,0:T(8,128)(2,1)} %kv_ref.1, bf16[64,2048]{1,0:T(8,128)(2,1)} %res_ref.1, ...), custom_call_target="tpu_custom_call" | custom-call | tf_op jit(solution)/shard_map/layer/pallas_call | solution.py:378
  153.6 1.7 %copy.18 = bf16[64,2048]{1,0:T(8,128)(2,1)} copy(bf16[64,2048]{1,0:T(8,128)(2,1)} %layer.1) | data formatting | bytes 524288
  (1 shorter events, 0.0 us)

commit v4 on v3

--- a/solution.py
+++ b/solution.py
@@ -210,47 +210,54 @@
             ).astype(jnp.bfloat16)
 
     first.start(0)
-    first.finish()
-    first.start(1)
     loads[0].wait()
     prefill(0)
     first.finish()
+    first.start(1)
+    prefill(1)
+    first.finish()
     first.start_last()
-    prefill(1)
     prefill(2)
     loads[1].wait()
     first.finish_last()
 
+    olds, news, pairs = [], [], []
     for s in range(DEC):
         src = request_ref[s]
         sz, sy, sx, sc = src // 128, (src // 32) % 4, (src // 8) % 4, (src // 4) % 2
         sr = src % 4
-        pair = a2[sz, sy, sx, sc, sr].astype(jnp.float32)
-        for g, (buf, target) in enumerate(((a0, s0), (a1, s1))):
+        pairs.append(a2[sz, sy, sx, sc, sr].astype(jnp.float32))
+        for g, buf in enumerate((a0, a1)):
             q = buf[sz, sy, sx, sc, sr]
+            old = dot_t(q, cache[0, s, :, g * HEAD:(g + 1) * HEAD]) * scale
+            position = lax.broadcasted_iota(jnp.int32, old.shape, 1)
+            olds.append(jnp.where(position < len_ref[s], old, MASKED))
+            own = q.astype(jnp.float32) * pairs[s][g:g + 1]
+            news.append(own.sum(axis=-1, keepdims=True) * scale)
+    old, new = jnp.concatenate(olds, axis=0), jnp.concatenate(news, axis=0)
+    top = jnp.maximum(old.max(axis=-1, keepdims=True), new)
+    old, new = jnp.exp(old - top), jnp.exp(new - top)
+    inv = 1.0 / (old.sum(axis=-1, keepdims=True) + new)
+    old = old * inv
+    new = (new * inv).astype(jnp.bfloat16).astype(jnp.float32)
+    for s in range(DEC):
+        for g, target in enumerate((s0, s1)):
+            part = slice((s * 2 + g) * GROUP, (s * 2 + g + 1) * GROUP)
             cols = slice(g * HEAD, (g + 1) * HEAD)
-            old = dot_t(q, cache[0, s, :, cols]) * scale
-            new = (q.astype(jnp.float32) * pair[g:g + 1]).sum(axis=-1, keepdims=True) * scale
-            position = lax.broadcasted_iota(jnp.int32, old.shape, 1)
-            old = jnp.where(position < len_ref[s], old, MASKED)
-            top = jnp.maximum(old.max(axis=-1, keepdims=True), new)
-            old, new = jnp.exp(old - top), jnp.exp(new - top)
-            inv = 1.0 / (old.sum(axis=-1, keepdims=True) + new)
-            out = dot_n((old * inv).astype(jnp.bfloat16), cache[1, s, :, cols])
-            own = (new * inv).astype(jnp.bfloat16).astype(jnp.float32)
-            result = (out + own * pair[2 + g:3 + g]).astype(jnp.bfloat16)
+            out = dot_n(old[part].astype(jnp.bfloat16), cache[1, s, :, cols])
+            result = (out + new[part] * pairs[s][2 + g:3 + g]).astype(jnp.bfloat16)
             if s < DEC - 1:
                 target[s] = result
             else:
                 s2[g] = result
 
     second.start(0)
+    routing()
     second.finish()
     second.start(1)
     prefill(3)
     second.finish()
     second.start_last()
-    routing()
     loads[2].wait()
     second.finish_last()
     for s in range(DEC):

time: 155 us -> 153 us (0.987)
  Pallas kernels: 152 us -> 150 us
    pallas_call x1, Pallas kernels: 152 us -> 150 us  [layer(): pl.pallas_call(layer_kernel, out_shape=jax.ShapeDtypeStruct((rows, width)...]
where the time goes in v4:
time: 153 us
  Pallas kernels  150 us (98%)
  local copies, waits for them, and re-layouts  1.67 us (1%)
    pallas_call x1, Pallas kernels, layer(): pl.pallas_call(layer_kernel, out_shape=jax.ShapeDtypeStruct((rows, width)...  150 us

profile of v4, /device:TPU:13, one launch (start us, length us, event | category | flops | bytes accessed | tf_op | source)
XLA Modules:
  0.0 153.3 jit_solution(18407636645514610336)
XLA Ops:
  0.7 1.4 select_reduce_fusion.request_ref
  2.0 149.5 %layer.1 = bf16[64,2048]{1,0:T(8,128)(2,1)} custom-call(s32[4]{0:T(128)} %select_reduce_fusion.request_ref, s32[512]{0:T(512)} %place_ref.1, s32[4]{0:T(128)} %len_ref.1, s32[1]{0:T(128)S(6)} %copy.17.prior_ref, bf16[64,2048]{1,0:T(8,128)(2,1)} %q_ref.1, bf16[2,64,256]{2,1,0:T(8,128)(2,1)} %kv_ref.1, bf16[64,2048]{1,0:T(8,128)(2,1)} %res_ref.1, ...), custom_call_target="tpu_custom_call" | custom-call | tf_op jit(solution)/shard_map/layer/pallas_call | solution.py:385
  151.6 1.7 %copy.18 = bf16[64,2048]{1,0:T(8,128)(2,1)} copy(bf16[64,2048]{1,0:T(8,128)(2,1)} %layer.1) | data formatting | bytes 524288
  (1 shorter events, 0.0 us)
